TPU v7x, 32 devices: a whole 2x2x4 slice. The times are simulated.
32 devices in a mesh: groups: 2 (over y), ctx: 4 (over z), head: 2 (over x), rep: 2 (over core).
Axes of the slice: x: 2, y: 2, z: 4, core: 2. Of those that a mesh axis runs over, the one named last changes fastest.
Arguments:
- queries: bfloat16 [8192, 16, 2, 128], P(('groups', 'ctx'), 'head', 'rep'), parts along dimension 0, may hold values from -10 to 10
- keys_values: bfloat16 [2, 8192, 16, 128], P('rep', ('groups', 'ctx'), 'head'), parts along dimension 1, may hold values from -6 to 6
- far_list: int32 [64, 16], P('groups'), parts along dimension 0, may hold values from 0 to 31, as said below
- far_count: int32 [64], P('groups'), parts along dimension 0, may hold values from 0 to 8
Outputs:
- attended: bfloat16 [8192, 16, 2, 128], P(('groups', 'ctx'), 'head', 'rep'), parts along dimension 0
There are 2 independent parts, one for each index of `groups`. A program takes and returns all parts, laid end to end along the dimension named above; each array names one. Nothing has to cross between parts.
Inputs may be any that keep to these rules, and one draw needn't show every extreme that they name: `far_list`: for query block c, the entries j < far_count[c] are distinct block numbers no later than c - 4; entries from far_count[c] on are arbitrary and not read. Taken over all query blocks of one span of 1024 tokens, the counted entries name at most 2 distinct blocks of any one span, and some span's query blocks name exactly 2 of some span in every draw.
All inputs are finite; a program needn't handle non-finite values.
Results may differ from a plain program's by a relative error of at most 0.003.
Values may be sent and summed in bfloat16 or wider, within the bound.
A program may use at most 128 MiB of HBM per device.

v0:
```python
import jax
import jax.numpy as jnp
from jax import lax
from jax.sharding import PartitionSpec as P

BLK = 128
WB = 4
FSEL = 16
CAP = 2
floor_score = -1e30
score_scale = 1.0 / 12.0


def partner(block, axis, stride):
    count = lax.axis_size(axis)
    route = []
    for low in range(count):
        high = low | 1 << stride
        if high != low and high < count:
            route += [(low, high), (high, low)]
    return lax.ppermute(block, axis, route)


def from_behind(x, axis, by):
    count = lax.axis_size(axis)
    pairs = [(i, i + by) for i in range(count) if 0 <= i + by < count]
    return lax.ppermute(x, axis, pairs)


def group_weights(scores, usable):
    masked = jnp.where(usable, scores, floor_score)
    summit = jnp.max(masked, axis=-1, keepdims=True)
    weights = jnp.where(usable, jnp.exp(masked - summit), 0.0)
    return (summit, weights, jnp.sum(weights, axis=-1, keepdims=True))


def row_major(stacked):
    return jnp.moveaxis(stacked, 0, 2).reshape(
        stacked.shape[1], stacked.shape[2], stacked.shape[0] * stacked.shape[3], stacked.shape[-1]
    )


def local(queries, keys_values, far_list, far_count):
    tok_rows, head_count, query_group, head_width = queries.shape
    block_len = BLK
    own_blocks = tok_rows // block_len
    span_count = lax.axis_size("ctx")
    my_span = lax.axis_index("ctx")
    my_side = lax.axis_index("rep")
    rim_len = (WB - 1) * block_len
    rim_start = tok_rows - rim_len
    other_half = partner(keys_values, "rep", 0)
    local_pair = jnp.concatenate(
        [
            jnp.where(my_side == 0, keys_values, other_half),
            jnp.where(my_side == 0, other_half, keys_values),
        ],
        axis=0,
    )
    slot_range = jnp.arange(FSEL, dtype=jnp.int32)
    block_index = jnp.arange(own_blocks, dtype=jnp.int32)
    my_blocks = my_span * own_blocks + block_index
    counted = slot_range[None, :] < far_count[:, None]
    every_block = jnp.arange(span_count * own_blocks, dtype=jnp.int32)
    list_blocks = far_list.reshape(span_count, own_blocks, FSEL)
    counted_blocks = counted.reshape(span_count, own_blocks, FSEL)
    flat_lists = list_blocks.reshape(span_count, -1)
    flat_counted = counted_blocks.reshape(span_count, -1)
    wanted = jnp.any(
        (flat_lists[:, :, None] == my_blocks[None, None, :]) & flat_counted[:, :, None], axis=1
    )
    wanted_rank = jnp.cumsum(wanted.astype(jnp.int32), axis=1) - 1
    in_slot = wanted[:, None, :] & (
        wanted_rank[:, None, :] == jnp.arange(CAP, dtype=jnp.int32)[None, :, None]
    )
    send_index = jnp.sum(jnp.where(in_slot, block_index[None, None, :], 0), axis=2).reshape(-1)
    slot_width = CAP
    rim_pair = from_behind(local_pair[:, rim_start:], "ctx", 1)
    blocked = local_pair.reshape(local_pair.shape[0], own_blocks, block_len, head_count, head_width)
    pool_pair = lax.all_to_all(
        jnp.take(blocked, send_index, axis=1), "ctx", split_axis=1, concat_axis=1, tiled=True
    )
    my_list = lax.dynamic_slice_in_dim(far_list, my_span * own_blocks, own_blocks, 0)
    my_count = lax.dynamic_slice_in_dim(far_count, my_span * own_blocks, own_blocks, 0)
    my_counted = slot_range[None, :] < my_count[:, None]
    extended = jnp.concatenate([rim_pair, local_pair], axis=1)
    query_rows = min(4 * block_len, tok_rows)
    key_rows = query_rows + rim_len
    base_pos = my_span * tok_rows

    def near_part(first_row):
        query_tile = lax.dynamic_slice_in_dim(queries, first_row, query_rows, 0)
        pair_tile = lax.dynamic_slice_in_dim(extended, first_row, key_rows, 1)
        scores = (
            jnp.einsum(
                "qhgd,khd->hgqk", query_tile, pair_tile[0], preferred_element_type=jnp.float32
            )
            * score_scale
        )
        query_pos = first_row + jnp.arange(query_rows, dtype=jnp.int32)
        key_pos = first_row - rim_len + jnp.arange(key_rows, dtype=jnp.int32)
        usable = (
            (key_pos[None, :] <= query_pos[:, None])
            & (key_pos[None, :] // block_len >= query_pos[:, None] // block_len - WB + 1)
            & (base_pos + key_pos[None, :] >= 0)
        )
        summit, weights, weight_sum = group_weights(scores, usable)
        mixed_out = jnp.einsum(
            "hgqk,khd->hgqd",
            weights.astype(jnp.bfloat16),
            pair_tile[1],
            preferred_element_type=jnp.float32,
        )
        return (summit, mixed_out, weight_sum)

    starts = jnp.arange(tok_rows // query_rows, dtype=jnp.int32) * query_rows
    near_top, near_out, near_sum = lax.map(near_part, starts)
    far_keys_len = FSEL * block_len
    query_blocks = queries.reshape(own_blocks, block_len, head_count, query_group, head_width)
    named_block = (my_list.reshape(-1)[:, None] == every_block[None, :]) & my_counted.reshape(-1)[
        :, None
    ]
    needed = jnp.any(named_block, axis=0).reshape(span_count, own_blocks)
    place = (
        jnp.cumsum(needed.astype(jnp.int32), axis=1)
        - 1
        + 0
        + jnp.arange(span_count, dtype=jnp.int32)[:, None] * slot_width
    )
    own_slots = jnp.sum(jnp.where(named_block, place.reshape(-1)[None, :], 0), axis=1).reshape(
        my_list.shape[0], FSEL
    )
    total = query_blocks.shape[0]
    width_step = 4
    turns = total // width_step

    def far_group(task):
        query_tile, slot_tile, live = task
        keys_tile = jnp.take(pool_pair[0], slot_tile.reshape(-1), axis=0).reshape(
            width_step, far_keys_len, head_count, head_width
        )
        value_tile = jnp.take(pool_pair[1], slot_tile.reshape(-1), axis=0).reshape(
            width_step, far_keys_len, head_count, head_width
        )
        scores = (
            jnp.einsum(
                "bqhgd,bkhd->bhgqk", query_tile, keys_tile, preferred_element_type=jnp.float32
            )
            * score_scale
        )
        usable = jnp.repeat(slot_range[None, :] < live[:, None], block_len, axis=1)[
            :, None, None, None, :
        ]
        summit, weights, weight_sum = group_weights(scores, usable)
        mixed_out = jnp.einsum(
            "bhgqk,bkhd->bhgqd",
            weights.astype(jnp.bfloat16),
            value_tile,
            preferred_element_type=jnp.float32,
        )
        return (summit, mixed_out, weight_sum)

    grouped = (
        query_blocks.reshape((turns, width_step) + query_blocks.shape[1:]),
        own_slots.reshape(turns, width_step, FSEL),
        my_count.reshape(turns, width_step),
    )
    results = lax.map(far_group, grouped)
    own_top, own_out, own_sum = tuple(
        (piece.reshape((total,) + piece.shape[2:]) for piece in results)
    )
    far_top, far_out, far_sum = (row_major(own_top), row_major(own_out), row_major(own_sum))
    near_top, near_out, near_sum = (row_major(near_top), row_major(near_out), row_major(near_sum))
    summit = jnp.maximum(near_top, far_top)
    near_scale = jnp.exp(near_top - summit)
    far_scale = jnp.exp(far_top - summit)
    result = (near_scale * near_out + far_scale * far_out) / (
        near_scale * near_sum + far_scale * far_sum
    )
    return jnp.transpose(result, (2, 0, 1, 3)).astype(jnp.bfloat16)


def solution(mesh):
    in_specs = (
        P(("groups", "ctx"), "head", "rep", None),
        P("rep", ("groups", "ctx"), "head", None),
        P("groups", None),
        P("groups"),
    )
    out_specs = P(("groups", "ctx"), "head", "rep", None)
    return jax.shard_map(local, mesh=mesh, in_specs=in_specs, out_specs=out_specs, check_vma=False)
```

profile of v0, /device:TPU:24, one launch (start us, length us, event | category | flops | bytes accessed | tf_op | source)
XLA Modules:
  0.0 359.6 jit_solution(871911679812161485)
XLA Ops:
  16.7 4.6 %copy.52 = bf16[2,1024,8,128]{3,2,1,0:T(8,128)(2,1)} copy(bf16[2,1024,8,128]{3,1,2,0:T(8,128)(2,1)S(1)} %pad_maximum_fusion) | data formatting | bytes 8388608 | tf_op jit(solution)/shard_map/concatenate | solution.py:53
  21.4 5.2 %gather_fusion.2 = bf16[8,2,128,8,128]{4,3,2,1,0:T(8,128)(2,1)} fusion(bf16[2,8,128,8,128]{4,3,2,1,0:T(8,128)(2,1)} %bitcast.197, s32[1024]{0:T(1024)S(1)} %pad_clamp_fusion.1), kind=kCustom, calls=%fused_computation.2 | custom fusion | bytes 8388640 | tf_op jit(solution)/shard_map/jit(_take)/gather | solution.py:81
  26.6 4.6 %select_bitcast_fusion = bf16[2,8,128,8,128]{4,3,2,0,1:T(8,128)(2,1)} fusion(bf16[8,2,128,8,128]{4,3,2,1,0:T(8,128)(2,1)} %gather_fusion.2, pred[8]{0:T(512)(128)(4,1)S(1)} %compare_and_fusion.1), kind=kLoop, calls=%fused_computation.88 | loop fusion | flops 2097152 | bytes 8388616 | tf_op jit(solution)/shard_map/jit(_take)/select_n | solution.py:81
  31.2 8.4 %all-to-all-start = ((bf16[2,8,128,8,128]{4,3,2,0,1:T(8,128)(2,1)}), bf16[2,8,128,8,128]{4,3,2,0,1:T(8,128)(2,1)}, u32[]{:S(2)}, u32[]{:S(2)}) async-start(bf16[2,8,128,8,128]{4,3,2,0,1:T(8,128)(2,1)} %select_bitcast_fusion), calls=%async_computation | async-start | bytes 8388608 | tf_op jit(solution)/shard_map/all_to_all | solution.py:80
  39.6 12.3 %collective-permute-done.1 = bf16[2,384,8,128]{3,1,2,0:T(8,128)(2,1)} collective-permute-done((bf16[2,384,8,128]{3,1,2,0:T(8,128)(2,1)}, bf16[2,384,8,128]{3,1,2,0:T(8,128)(2,1)}, u32[]{:S(2)}, u32[]{:S(2)}) %collective-permute-start.1) | collective-permute-done | bytes 1572896 | tf_op jit(solution)/shard_map/ppermute | solution.py:27
  52.0 4.9 %maximum_maximum_fusion = bf16[2,1408,8,128]{3,1,2,0:T(8,128)(2,1)} fusion(bf16[1,1024,8,128]{3,1,2,0:T(8,128)(2,1)} %copy-done.1, bf16[1,1024,8,128]{3,1,2,0:T(8,128)(2,1)S(1)} %get-tuple-element.367, bf16[2,384,8,128]{3,1,2,0:T(8,128)(2,1)} %collective-permute-done.1), kind=kLoop, calls=%fused_computation.84 | loop fusion | flops 17301504 | bytes 11534336 | tf_op jit(solution)/shard_map/concatenate | solution.py:86
  56.9 72.9 %while.34 = (s32[]{:T(128)}, f32[2,8,1,512,1]{3,1,4,2,0:T(8,128)S(1)}, f32[2,8,1,512,128]{4,3,1,2,0:T(8,128)}, f32[2,8,1,512,1]{3,4,2,1,0:T(1,128)S(1)}, s32[2]{...) while((s32[]{:T(128)}, ...), condition=%wide.region_3.4_spmd, body=%wide.region_0.3_spmd.sunk | while | flops 1928610944 | bytes 54944268 | solution.py:117
  64.2 8.4 %fusion.67 = (f32[8,512]{1,0:T(8,128)S(1)}, f32[8,896,512]{2,1,0:T(8,128)}) fusion(pred[512,896]{0,1:T(8,128)(4,1)S(1)} %and_and_fusion.2, bf16[512,8,1,128]{3,1,2,0:T(8,128)(2,1)S(1)} %constant_dynamic-slice_fusion.8, bf16[2,1408,8,128]{3,1,2,0:T(8,128)(2,1)} %get-tuple-element.552, s32[]{:T(128)S(6)} %select_n.250), kind=kOutput, calls=%fused_computation.6.clone.1 | convolution fusion | flops 950530048 | bytes 18038788 | tf_op jit(solution)/shard_map/while/body/eval_jaxpr/qhgd,khd->hgqk/dot_general | solution.py:95
  72.6 8.7 %fusion.68 = f32[8,512]{1,0:T(8,128)S(1)} fusion(f32[8,896,512]{2,1,0:T(8,128)} %get-tuple-element.476, f32[8,512]{1,0:T(8,128)S(1)} %get-tuple-element.475, pred[512,896]{0,1:T(8,128)(4,1)S(1)} %and_and_fusion.2), kind=kLoop, calls=%fused_computation.7.clone.1 | loop fusion | flops 18345984 | bytes 15171584 | tf_op jit(solution)/shard_map/while/body/eval_jaxpr/reduce_sum | solution.py:34
  81.3 12.1 %bitcast_dynamic-update-slice_fusion.9 = f32[2,8,1,512,128]{4,3,1,2,0:T(8,128)} fusion(f32[2,8,1,512,128]{4,3,1,2,0:T(8,128)} %get-tuple-element.534, s32[]{:T(128)} %get-tuple-element.532, bf16[2,1408,8,128]{3,1,2,0:T(8,128)(2,1)} %get-tuple-element.552, s32[]{:T(128)S(6)} %add.369, s32[]{:T(128)S(6)} %select_n.250, ...), kind=kOutput, calls=%fused_computation.12.clone.1 | convolution fusion | flops 957874176 | bytes 19087880 | tf_op jit(solution)/shard_map/while/body/eval_jaxpr/hgqk,khd->hgqd/dot_general | solution.py:108
  100.7 8.4 %fusion.67 = (f32[8,512]{1,0:T(8,128)S(1)}, f32[8,896,512]{2,1,0:T(8,128)}) fusion(pred[512,896]{0,1:T(8,128)(4,1)S(1)} %and_and_fusion.2, bf16[512,8,1,128]{3,1,2,0:T(8,128)(2,1)S(1)} %constant_dynamic-slice_fusion.8, bf16[2,1408,8,128]{3,1,2,0:T(8,128)(2,1)} %get-tuple-element.552, s32[]{:T(128)S(6)} %select_n.250), kind=kOutput, calls=%fused_computation.6.clone.1 | convolution fusion | flops 950530048 | bytes 18038788 | tf_op jit(solution)/shard_map/while/body/eval_jaxpr/qhgd,khd->hgqk/dot_general | solution.py:95
  109.1 8.7 %fusion.68 = f32[8,512]{1,0:T(8,128)S(1)} fusion(f32[8,896,512]{2,1,0:T(8,128)} %get-tuple-element.476, f32[8,512]{1,0:T(8,128)S(1)} %get-tuple-element.475, pred[512,896]{0,1:T(8,128)(4,1)S(1)} %and_and_fusion.2), kind=kLoop, calls=%fused_computation.7.clone.1 | loop fusion | flops 18345984 | bytes 15171584 | tf_op jit(solution)/shard_map/while/body/eval_jaxpr/reduce_sum | solution.py:34
  117.8 12.0 %bitcast_dynamic-update-slice_fusion.9 = f32[2,8,1,512,128]{4,3,1,2,0:T(8,128)} fusion(f32[2,8,1,512,128]{4,3,1,2,0:T(8,128)} %get-tuple-element.534, s32[]{:T(128)} %get-tuple-element.532, bf16[2,1408,8,128]{3,1,2,0:T(8,128)(2,1)} %get-tuple-element.552, s32[]{:T(128)S(6)} %add.369, s32[]{:T(128)S(6)} %select_n.250, ...), kind=kOutput, calls=%fused_computation.12.clone.1 | convolution fusion | flops 957874176 | bytes 19087880 | tf_op jit(solution)/shard_map/while/body/eval_jaxpr/hgqk,khd->hgqd/dot_general | solution.py:108
  130.4 6.5 %copy.59 = f32[8,1,2,512,128]{4,0,3,2,1:T(8,128)} copy(f32[8,1,2,512,128]{4,3,0,1,2:T(8,128)} %bitcast.198) | data formatting | bytes 8388608 | tf_op jit(solution)/shard_map/transpose | solution.py:38
  137.0 4.3 %all-to-all-done = bf16[2,8,128,8,128]{4,3,2,0,1:T(8,128)(2,1)} async-done(((bf16[2,8,128,8,128]{4,3,2,0,1:T(8,128)(2,1)}), bf16[2,8,128,8,128]{4,3,2,0,1:T(8,128)(2,1)}, u32[]{:S(2)}, u32[]{:S(2)}) %all-to-all-start) | async-done | bytes 4194336 | tf_op jit(solution)/shard_map/all_to_all | solution.py:80
  141.2 4.5 %copy.56 = bf16[2,8,128,8,128]{4,3,2,1,0:T(8,128)(2,1)} copy(bf16[2,8,128,8,128]{4,3,2,0,1:T(8,128)(2,1)} %all-to-all-done) | data formatting | bytes 8388608
  145.8 202.6 %while.35 = (s32[]{:T(128)}, f32[2,4,8,1,128,1]{4,2,1,5,3,0:T(8,128)S(1)}, f32[2,4,8,1,128,128]{5,4,2,1,3,0:T(8,128)}, f32[2,4,8,1,128,1]{4,5,3,2,1,0:T(1,128)S(...) while((s32[]{:T(128)}, ...), condition=%wide.region_13.15_spmd.clone, body=%wide.region_10.14_spmd.clone.sunk | while | flops 4420789760 | bytes 290651552 | solution.py:168
  145.9 3.9 %slice_bitcast_fusion.3 = (bf16[8,128,8,128]{3,2,1,0:T(8,128)(2,1)}, bf16[8,128,8,128]{3,2,1,0:T(8,128)(2,1)S(1)}) fusion(bf16[2,8,128,8,128]{4,3,2,1,0:T(8,128)(2,1)} %get-tuple-element.514), kind=kLoop, calls=%fused_computation.66.clone.1 | loop fusion | bytes 8388608 | tf_op jit(solution)/shard_map/while/body/eval_jaxpr/squeeze | solution.py:142
  149.8 8.9 %gather_fusion = bf16[64,128,8,128]{3,2,1,0:T(8,128)(2,1)} fusion(bf16[8,128,8,128]{3,2,1,0:T(8,128)(2,1)} %get-tuple-element.485, s32[1024]{0:T(1024)S(1)} %pad_clamp_fusion.3), kind=kCustom, calls=%fused_computation.1.clone.clone.1 | custom fusion | bytes 33554688 | tf_op jit(solution)/shard_map/while/body/eval_jaxpr/jit(_take)/gather | solution.py:142
  158.7 7.3 %gather_fusion.1 = bf16[64,128,8,128]{3,2,1,0:T(8,128)(2,1)} fusion(bf16[8,128,8,128]{3,2,1,0:T(8,128)(2,1)S(1)} %get-tuple-element.486, s32[1024]{0:T(1024)S(1)} %pad_clamp_fusion.3), kind=kCustom, calls=%fused_computation.clone.clone.1 | custom fusion | bytes 33554688 | tf_op jit(solution)/shard_map/while/body/eval_jaxpr/jit(_take)/gather | solution.py:139
  166.0 23.2 %broadcast_select_fusion.5 = (bf16[64,128,8,128]{3,2,1,0:T(8,128)(2,1)}, bf16[64,128,8,128]{3,2,1,0:T(8,128)(2,1)}) fusion(bf16[64,128,8,128]{3,2,1,0:T(8,128)(2,1)} %gather_fusion, pred[64]{0:T(512)(128)(4,1)S(1)} %compare_and_fusion.3, bf16[64,128,8,128]{3,2,1,0:T(8,128)(2,1)} %gather_fusion.1), kind=kLoop, calls=%fused_computation.61.clone.1 | loop fusion | flops 16777216 | bytes 67108928 | tf_op jit(solution)/shard_map/while/body/eval_jaxpr/jit(_take)/select_n | solution.py:142
  189.5 19.7 %bitcast_reduce_fusion.2 = (f32[4,8,128]{2,1,0:T(8,128)S(1)}, f32[4,8,2048,128]{3,2,1,0:T(8,128)}) fusion(pred[4,2048]{1,0:T(4,128)(4,1)S(1)} %bitcast.199, bf16[1,4,128,8,1,128]{5,3,2,1,0,4:T(8,128)(2,1)S(1)} %constant_dynamic-slice_fusion.9, bf16[4,2048,8,128]{3,2,1,0:T(8,128)(2,1)} %bitcast.193), kind=kOutput, calls=%fused_computation.47.clone.1 | convolution fusion | flops 2172645376 | bytes 51404800 | tf_op jit(solution)/shard_map/while/body/eval_jaxpr/bqhgd,bkhd->bhgqk/dot_general | solution.py:146
  209.2 15.1 %fusion.72 = f32[4,8,128]{2,1,0:T(8,128)S(1)} fusion(f32[4,8,2048,128]{3,2,1,0:T(8,128)} %get-tuple-element.490, f32[4,8,128]{2,1,0:T(8,128)S(1)} %get-tuple-element.488, pred[4,2048]{1,0:T(4,128)(4,1)S(1)} %bitcast.200), kind=kLoop, calls=%fused_computation.51.clone.1 | loop fusion | flops 41938944 | bytes 33595392 | tf_op jit(solution)/shard_map/while/body/eval_jaxpr/reduce_sum | solution.py:34
  224.3 22.7 %bitcast_dynamic-update-slice_fusion.11 = f32[2,4,8,1,128,128]{5,4,2,1,3,0:T(8,128)} fusion(f32[2,4,8,1,128,128]{5,4,2,1,3,0:T(8,128)} %get-tuple-element.502, s32[]{:T(128)} %get-tuple-element.500, bf16[4,2048,8,128]{3,2,1,0:T(8,128)(2,1)} %bitcast.192, f32[4,8,2048,128]{3,2,1,0:T(8,128)} %get-tuple-element.490, ...), kind=kOutput, calls=%fused_computation.65.clone.1 | convolution fusion | flops 2189426688 | bytes 52462080 | tf_op jit(solution)/shard_map/while/body/eval_jaxpr/bhgqk,bkhd->bhgqd/dot_general | solution.py:155
  251.1 8.9 %gather_fusion = bf16[64,128,8,128]{3,2,1,0:T(8,128)(2,1)} fusion(bf16[8,128,8,128]{3,2,1,0:T(8,128)(2,1)} %get-tuple-element.485, s32[1024]{0:T(1024)S(1)} %pad_clamp_fusion.3), kind=kCustom, calls=%fused_computation.1.clone.clone.1 | custom fusion | bytes 33554688 | tf_op jit(solution)/shard_map/while/body/eval_jaxpr/jit(_take)/gather | solution.py:142
  260.0 7.4 %gather_fusion.1 = bf16[64,128,8,128]{3,2,1,0:T(8,128)(2,1)} fusion(bf16[8,128,8,128]{3,2,1,0:T(8,128)(2,1)S(1)} %get-tuple-element.486, s32[1024]{0:T(1024)S(1)} %pad_clamp_fusion.3), kind=kCustom, calls=%fused_computation.clone.clone.1 | custom fusion | bytes 33554688 | tf_op jit(solution)/shard_map/while/body/eval_jaxpr/jit(_take)/gather | solution.py:139
  267.4 23.2 %broadcast_select_fusion.5 = (bf16[64,128,8,128]{3,2,1,0:T(8,128)(2,1)}, bf16[64,128,8,128]{3,2,1,0:T(8,128)(2,1)}) fusion(bf16[64,128,8,128]{3,2,1,0:T(8,128)(2,1)} %gather_fusion, pred[64]{0:T(512)(128)(4,1)S(1)} %compare_and_fusion.3, bf16[64,128,8,128]{3,2,1,0:T(8,128)(2,1)} %gather_fusion.1), kind=kLoop, calls=%fused_computation.61.clone.1 | loop fusion | flops 16777216 | bytes 67108928 | tf_op jit(solution)/shard_map/while/body/eval_jaxpr/jit(_take)/select_n | solution.py:142
  290.8 19.7 %bitcast_reduce_fusion.2 = (f32[4,8,128]{2,1,0:T(8,128)S(1)}, f32[4,8,2048,128]{3,2,1,0:T(8,128)}) fusion(pred[4,2048]{1,0:T(4,128)(4,1)S(1)} %bitcast.199, bf16[1,4,128,8,1,128]{5,3,2,1,0,4:T(8,128)(2,1)S(1)} %constant_dynamic-slice_fusion.9, bf16[4,2048,8,128]{3,2,1,0:T(8,128)(2,1)} %bitcast.193), kind=kOutput, calls=%fused_computation.47.clone.1 | convolution fusion | flops 2172645376 | bytes 51404800 | tf_op jit(solution)/shard_map/while/body/eval_jaxpr/bqhgd,bkhd->bhgqk/dot_general | solution.py:146
  310.5 15.1 %fusion.72 = f32[4,8,128]{2,1,0:T(8,128)S(1)} fusion(f32[4,8,2048,128]{3,2,1,0:T(8,128)} %get-tuple-element.490, f32[4,8,128]{2,1,0:T(8,128)S(1)} %get-tuple-element.488, pred[4,2048]{1,0:T(4,128)(4,1)S(1)} %bitcast.200), kind=kLoop, calls=%fused_computation.51.clone.1 | loop fusion | flops 41938944 | bytes 33595392 | tf_op jit(solution)/shard_map/while/body/eval_jaxpr/reduce_sum | solution.py:34
  325.7 22.7 %bitcast_dynamic-update-slice_fusion.11 = f32[2,4,8,1,128,128]{5,4,2,1,3,0:T(8,128)} fusion(f32[2,4,8,1,128,128]{5,4,2,1,3,0:T(8,128)} %get-tuple-element.502, s32[]{:T(128)} %get-tuple-element.500, bf16[4,2048,8,128]{3,2,1,0:T(8,128)(2,1)} %bitcast.192, f32[4,8,2048,128]{3,2,1,0:T(8,128)} %get-tuple-element.490, ...), kind=kOutput, calls=%fused_computation.65.clone.1 | convolution fusion | flops 2189426688 | bytes 52462080 | tf_op jit(solution)/shard_map/while/body/eval_jaxpr/bhgqk,bkhd->bhgqd/dot_general | solution.py:155
  349.1 4.7 %copy.61 = f32[8,8,1,128,128]{4,1,3,0,2:T(8,128)S(1)} copy(f32[8,8,1,128,128]{4,3,1,0,2:T(8,128)} %bitcast.24) | data formatting | bytes 8388608 | tf_op jit(solution)/shard_map/reshape | solution.py:170
  353.8 5.8 %fusion.47 = bf16[1024,8,1,128]{3,1,2,0:T(8,128)(2,1)} fusion(f32[8,1024]{0,1:T(8,128)S(1)} %copy.63, f32[8,1,1024,128]{3,0,1,2:T(8,128)S(1)} %bitcast.196, f32[8,1024]{0,1:T(8,128)S(1)} %copy.60, f32[8,1,1024,128]{3,0,1,2:T(8,128)S(1)} %bitcast.195, f32[8,1024]{0,1:T(8,128)S(1)} %copy.58), kind=kLoop, calls=%fused_computation.90 | loop fusion | flops 5242880 | bytes 10584064 | tf_op jit(solution)/shard_map/convert_element_type | solution.py:180
  (115 shorter events, 29.5 us)
Async XLA Ops:
  1.9 5.1 %collective-permute-start = (bf16[1,1024,8,128]{3,1,2,0:T(8,128)(2,1)S(1)}, bf16[1,1024,8,128]{3,1,2,0:T(8,128)(2,1)}, u32[]{:S(2)}, u32[]{:S(2)}) collective-permute-start(bf16[1,1024,8,128]{3,1,2,0:T(8,128)(2,1)S(1)} %copy.46), channel_id=1, source_target_pairs={{0,1},{1,0},{2,3},{3,2},{4,5},{5,4},{6,7},{7,6},{8,9},{9,8},{10,11... | collective-permute-start | bytes 6291464 | tf_op jit(solution)/shard_map/ppermute | solution.py:21
  9.8 1.3 copy-start.1
  12.5 39.5 %collective-permute-start.1 = (bf16[2,384,8,128]{3,1,2,0:T(8,128)(2,1)}, bf16[2,384,8,128]{3,1,2,0:T(8,128)(2,1)}, u32[]{:S(2)}, u32[]{:S(2)}) collective-permute-start(bf16[2,384,8,128]{3,1,2,0:T(8,128)(2,1)} %fusion.48), channel_id=1, source_target_pairs={{0,4},{4,8},{8,12},{1,5},{5,9},{9,13},{2,6},{6,10},{10,14},{3,7},{... | collective-permute-start | bytes 4718600 | tf_op jit(solution)/shard_map/ppermute | solution.py:27
  14.1 0.6 copy-start.3
  31.2 110.0 %all-to-all-start = ((bf16[2,8,128,8,128]{4,3,2,0,1:T(8,128)(2,1)}), bf16[2,8,128,8,128]{4,3,2,0,1:T(8,128)(2,1)}, u32[]{:S(2)}, u32[]{:S(2)}) async-start(bf16[2,8,128,8,128]{4,3,2,0,1:T(8,128)(2,1)} %select_bitcast_fusion), calls=%async_computation | async-start | bytes 8388608 | tf_op jit(solution)/shard_map/all_to_all | solution.py:80
  129.8 16.0 %copy-start.6 = (f32[2,8,1,512,1]{3,1,4,2,0:T(8,128)}, f32[2,8,1,512,1]{3,1,4,2,0:T(8,128)S(1)}, u32[]{:S(2)}) copy-start(f32[2,8,1,512,1]{3,1,4,2,0:T(8,128)S(1)} %get-tuple-element.248) | copy-start | bytes 98308
  137.0 8.8 %copy-start.4 = (f32[2,4,8,1,128,1]{4,2,1,5,3,0:T(8,128)S(1)}, f32[2,4,8,1,128,1]{4,2,1,5,3,0:T(8,128)}, u32[]{:S(2)}) copy-start(f32[2,4,8,1,128,1]{4,2,1,5,3,0:T(8,128)} %copy-done.3) | copy-start | bytes 98308
  145.8 202.6 %copy-start.5 = (f32[1,8,2,512]{3,1,2,0:T(8,128)S(1)}, f32[1,8,2,512]{3,1,2,0:T(8,128)}, u32[]{:S(2)}) copy-start(f32[1,8,2,512]{3,1,2,0:T(8,128)} %copy.69) | copy-start | bytes 98308
  145.8 202.6 %copy-start.7 = (f32[2,8,1,512,1]{3,1,4,2,0:T(8,128)S(1)}, f32[2,8,1,512,1]{3,1,4,2,0:T(8,128)}, u32[]{:S(2)}) copy-start(f32[2,8,1,512,1]{3,1,4,2,0:T(8,128)} %copy-done.6) | copy-start | bytes 98308
  166.0 23.4 %copy-start = (bf16[2,4,128,8,1,128]{5,3,2,1,0,4:T(8,128)(2,1)S(1)}, bf16[2,4,128,8,1,128]{5,3,2,1,0,4:T(8,128)(2,1)}, u32[]{:S(2)}) copy-start(bf16[2,4,128,8,1,128]{5,3,2,1,0,4:T(8,128)(2,1)} %get-tuple-element.516) | copy-start | bytes 6291460 | tf_op jit(solution)/shard_map/while
  267.4 23.4 %copy-start = (bf16[2,4,128,8,1,128]{5,3,2,1,0,4:T(8,128)(2,1)S(1)}, bf16[2,4,128,8,1,128]{5,3,2,1,0,4:T(8,128)(2,1)}, u32[]{:S(2)}) copy-start(bf16[2,4,128,8,1,128]{5,3,2,1,0,4:T(8,128)(2,1)} %get-tuple-element.516) | copy-start | bytes 6291460 | tf_op jit(solution)/shard_map/while
  349.1 4.7 %copy-start.2 = (f32[8,1,2,512,128]{4,0,3,2,1:T(8,128)S(1)}, f32[8,1,2,512,128]{4,0,3,2,1:T(8,128)}, u32[]{:S(2)}) copy-start(f32[8,1,2,512,128]{4,0,3,2,1:T(8,128)} %copy.59) | copy-start | bytes 12582916
where the time goes:
time: 361 us; the launch traced here: 360 us
  matrix products  126 us (35%)
  other arithmetic  120 us (33%)
  local copies, waits for them, and re-layouts  79.6 us (22%)
  waiting for transfers between devices  16.6 us (5%)
  starting transfers between devices  9.72 us (3%)
  loops' own time  7.96 us (2%)
    reduce_sum x4, other arithmetic, group_weights(): return (summit, weights, jnp.sum(weights, axis=-1, keepdims=True))  47.6 us
    select_n x2, other arithmetic, far_group(): jnp.take(pool_pair[1], slot_tile.reshape(-1), axis=0)  46.4 us
    dot_general x2, matrix products, far_group(): jnp.einsum('bhgqk,bkhd->bhgqd', weights.astype(jnp.bfloat16), value_tile,...  45.4 us
    dot_general x2, matrix products, far_group(): jnp.einsum('bqhgd,bkhd->bhgqk', query_tile, keys_tile, preferred_element_...  39.4 us
    dot_general x2, matrix products, near_part(): jnp.einsum('hgqk,khd->hgqd', weights.astype(jnp.bfloat16), pair_tile[1],...  24 us
    gather x2, local copies, waits for them, and re-layouts, far_group(): jnp.take(pool_pair[1], slot_tile.reshape(-1), axis=0)  17.8 us
    dot_general x2, matrix products, near_part(): jnp.einsum('qhgd,khd->hgqk', query_tile, pair_tile[0], preferred_element_...  16.8 us
    gather x2, local copies, waits for them, and re-layouts, far_group(): jnp.take(pool_pair[0], slot_tile.reshape(-1), axis=0)  14.6 us
  transfers between devices with their start and end apart: 3, of which 2 were waited for; matrix products, arithmetic and copies ran while one was open for 28% of the time, Pallas kernels for 0%

commit v1 on v0

--- a/solution.py
+++ b/solution.py
@@ -77,8 +77,16 @@
     slot_width = CAP
     rim_pair = from_behind(local_pair[:, rim_start:], "ctx", 1)
     blocked = local_pair.reshape(local_pair.shape[0], own_blocks, block_len, head_count, head_width)
-    pool_pair = lax.all_to_all(
-        jnp.take(blocked, send_index, axis=1), "ctx", split_axis=1, concat_axis=1, tiled=True
+    pool_pair = jnp.concatenate(
+        lax.all_to_all(
+            jnp.stack(
+                jnp.split(jnp.take(blocked, send_index, axis=1), lax.axis_size("ctx"), axis=1)
+            ),
+            "ctx",
+            0,
+            0,
+        ),
+        axis=1,
     )
     my_list = lax.dynamic_slice_in_dim(far_list, my_span * own_blocks, own_blocks, 0)
     my_count = lax.dynamic_slice_in_dim(far_count, my_span * own_blocks, own_blocks, 0)

time: 361 us -> 372 us (1.030); the launches traced: 360 us -> 365 us
  loops' own time: 7.96 us -> 17.9 us
    another operation x1, loops' own time: 7.85 us -> 17.8 us  [local(): near_top, near_out, near_sum = lax.map(near_part, starts)]
    all_to_all x1, waiting for transfers between devices: 4.25 us -> 0.01 us  [local(): lax.all_to_all(jnp.stack(jnp.split(jnp.take(blocked, send_index, axis=1),...]
  transfers between devices with their start and end apart: 3 -> 3, of which waited for: 2 -> 1; matrix products, arithmetic and copies ran while one was open for 28% -> 27% of each run, Pallas kernels for 0% -> 0%
where the time goes in v1:
time: 372 us; the launch traced here: 365 us
  matrix products  126 us (34%)
  other arithmetic  119 us (32%)
  local copies, waits for them, and re-layouts  78.6 us (21%)
  loops' own time  17.9 us (5%)
  waiting for transfers between devices  13.8 us (4%)
  starting transfers between devices  10.2 us (3%)
    reduce_sum x4, other arithmetic, group_weights(): return (summit, weights, jnp.sum(weights, axis=-1, keepdims=True))  47.6 us
    select_n x2, other arithmetic, far_group(): jnp.take(pool_pair[1], slot_tile.reshape(-1), axis=0)  46.4 us
    dot_general x2, matrix products, far_group(): jnp.einsum('bhgqk,bkhd->bhgqd', weights.astype(jnp.bfloat16), value_tile,...  45.4 us
    dot_general x2, matrix products, far_group(): jnp.einsum('bqhgd,bkhd->bhgqk', query_tile, keys_tile, preferred_element_...  39.4 us
    dot_general x2, matrix products, near_part(): jnp.einsum('hgqk,khd->hgqd', weights.astype(jnp.bfloat16), pair_tile[1],...  24.1 us
    gather x2, local copies, waits for them, and re-layouts, far_group(): jnp.take(pool_pair[1], slot_tile.reshape(-1), axis=0)  17.8 us
    another operation x1, loops' own time, local(): near_top, near_out, near_sum = lax.map(near_part, starts)  17.8 us
    dot_general x2, matrix products, near_part(): jnp.einsum('qhgd,khd->hgqk', query_tile, pair_tile[0], preferred_element_...  16.8 us
  transfers between devices with their start and end apart: 3, of which 1 were waited for; matrix products, arithmetic and copies ran while one was open for 27% of the time, Pallas kernels for 0%

profile of v1, /device:TPU:24, one launch (start us, length us, event | category | flops | bytes accessed | tf_op | source)
XLA Modules:
  0.0 365.3 jit_solution(6261218820661865833)
XLA Ops:
  8.0 2.9 broadcast_select_fusion.3
  13.9 4.6 %copy.55 = bf16[2,1024,8,128]{3,2,1,0:T(8,128)(2,1)} copy(bf16[2,1024,8,128]{3,1,2,0:T(8,128)(2,1)S(1)} %pad_maximum_fusion) | data formatting | bytes 8388608 | tf_op jit(solution)/shard_map/concatenate | solution.py:53
  18.6 5.2 %gather_fusion.2 = bf16[8,2,128,8,128]{4,3,2,1,0:T(8,128)(2,1)} fusion(bf16[2,8,128,8,128]{4,3,2,1,0:T(8,128)(2,1)} %bitcast.208, s32[1024]{0:T(1024)S(1)} %pad_clamp_fusion.1), kind=kCustom, calls=%fused_computation.2 | custom fusion | bytes 8388640 | tf_op jit(solution)/shard_map/jit(_take)/gather | solution.py:83
  29.1 8.8 %all-to-all-start = ((bf16[4,2,2,128,8,128]{5,4,3,1,2,0:T(8,128)(2,1)}), bf16[4,2,2,128,8,128]{5,4,3,1,2,0:T(8,128)(2,1)}, u32[]{:S(2)}, u32[]{:S(2)}) async-start(bf16[4,2,2,128,8,128]{5,4,3,1,2,0:T(8,128)(2,1)} %pad_maximum_fusion.1), calls=%async_computation | async-start | bytes 8388608 | tf_op jit(solution)/shard_map/all_to_all | solution.py:81
  37.9 13.8 %collective-permute-done.1 = bf16[2,384,8,128]{3,1,2,0:T(8,128)(2,1)} collective-permute-done((bf16[2,384,8,128]{3,1,2,0:T(8,128)(2,1)}, bf16[2,384,8,128]{3,1,2,0:T(8,128)(2,1)}, u32[]{:S(2)}, u32[]{:S(2)}) %collective-permute-start.1) | collective-permute-done | bytes 1572896 | tf_op jit(solution)/shard_map/ppermute | solution.py:27
  51.7 4.9 %maximum_maximum_fusion = bf16[2,1408,8,128]{3,1,2,0:T(8,128)(2,1)} fusion(bf16[1,1024,8,128]{3,1,2,0:T(8,128)(2,1)} %copy-done.1, bf16[1,1024,8,128]{3,1,2,0:T(8,128)(2,1)S(1)} %get-tuple-element.371, bf16[2,384,8,128]{3,1,2,0:T(8,128)(2,1)} %collective-permute-done.1), kind=kLoop, calls=%fused_computation.84 | loop fusion | flops 17301504 | bytes 11534336 | tf_op jit(solution)/shard_map/concatenate | solution.py:94
  56.6 82.9 %while.34 = (s32[]{:T(128)}, f32[2,8,1,512,1]{3,1,4,2,0:T(8,128)S(1)}, f32[2,8,1,512,128]{4,3,1,2,0:T(8,128)}, f32[2,8,1,512,1]{3,4,2,1,0:T(1,128)S(1)}, s32[2]{...) while((s32[]{:T(128)}, ...), condition=%wide.region_3.4_spmd, body=%wide.region_0.3_spmd.sunk | while | flops 1928610944 | bytes 54944268 | solution.py:125
  64.0 8.4 %fusion.67 = (f32[8,512]{1,0:T(8,128)S(1)}, f32[8,896,512]{2,1,0:T(8,128)}) fusion(pred[512,896]{0,1:T(8,128)(4,1)S(1)} %and_and_fusion.2, bf16[512,8,1,128]{3,1,2,0:T(8,128)(2,1)S(1)} %constant_dynamic-slice_fusion.8, bf16[2,1408,8,128]{3,1,2,0:T(8,128)(2,1)} %get-tuple-element.556, s32[]{:T(128)S(6)} %select_n.250), kind=kOutput, calls=%fused_computation.6.clone.1 | convolution fusion | flops 950530048 | bytes 18038788 | tf_op jit(solution)/shard_map/while/body/eval_jaxpr/qhgd,khd->hgqk/dot_general | solution.py:103
  72.4 8.7 %fusion.68 = f32[8,512]{1,0:T(8,128)S(1)} fusion(f32[8,896,512]{2,1,0:T(8,128)} %get-tuple-element.480, f32[8,512]{1,0:T(8,128)S(1)} %get-tuple-element.479, pred[512,896]{0,1:T(8,128)(4,1)S(1)} %and_and_fusion.2), kind=kLoop, calls=%fused_computation.7.clone.1 | loop fusion | flops 18345984 | bytes 15171584 | tf_op jit(solution)/shard_map/while/body/eval_jaxpr/reduce_sum | solution.py:34
  81.1 12.1 %bitcast_dynamic-update-slice_fusion.9 = f32[2,8,1,512,128]{4,3,1,2,0:T(8,128)} fusion(f32[2,8,1,512,128]{4,3,1,2,0:T(8,128)} %get-tuple-element.538, s32[]{:T(128)} %get-tuple-element.536, bf16[2,1408,8,128]{3,1,2,0:T(8,128)(2,1)} %get-tuple-element.556, s32[]{:T(128)S(6)} %add.369, s32[]{:T(128)S(6)} %select_n.250, ...), kind=kOutput, calls=%fused_computation.12.clone.1 | convolution fusion | flops 957874176 | bytes 19087880 | tf_op jit(solution)/shard_map/while/body/eval_jaxpr/hgqk,khd->hgqd/dot_general | solution.py:116
  100.5 8.4 %fusion.67 = (f32[8,512]{1,0:T(8,128)S(1)}, f32[8,896,512]{2,1,0:T(8,128)}) fusion(pred[512,896]{0,1:T(8,128)(4,1)S(1)} %and_and_fusion.2, bf16[512,8,1,128]{3,1,2,0:T(8,128)(2,1)S(1)} %constant_dynamic-slice_fusion.8, bf16[2,1408,8,128]{3,1,2,0:T(8,128)(2,1)} %get-tuple-element.556, s32[]{:T(128)S(6)} %select_n.250), kind=kOutput, calls=%fused_computation.6.clone.1 | convolution fusion | flops 950530048 | bytes 18038788 | tf_op jit(solution)/shard_map/while/body/eval_jaxpr/qhgd,khd->hgqk/dot_general | solution.py:103
  108.9 8.7 %fusion.68 = f32[8,512]{1,0:T(8,128)S(1)} fusion(f32[8,896,512]{2,1,0:T(8,128)} %get-tuple-element.480, f32[8,512]{1,0:T(8,128)S(1)} %get-tuple-element.479, pred[512,896]{0,1:T(8,128)(4,1)S(1)} %and_and_fusion.2), kind=kLoop, calls=%fused_computation.7.clone.1 | loop fusion | flops 18345984 | bytes 15171584 | tf_op jit(solution)/shard_map/while/body/eval_jaxpr/reduce_sum | solution.py:34
  117.6 12.0 %bitcast_dynamic-update-slice_fusion.9 = f32[2,8,1,512,128]{4,3,1,2,0:T(8,128)} fusion(f32[2,8,1,512,128]{4,3,1,2,0:T(8,128)} %get-tuple-element.538, s32[]{:T(128)} %get-tuple-element.536, bf16[2,1408,8,128]{3,1,2,0:T(8,128)(2,1)} %get-tuple-element.556, s32[]{:T(128)S(6)} %add.369, s32[]{:T(128)S(6)} %select_n.250, ...), kind=kOutput, calls=%fused_computation.12.clone.1 | convolution fusion | flops 957874176 | bytes 19087880 | tf_op jit(solution)/shard_map/while/body/eval_jaxpr/hgqk,khd->hgqd/dot_general | solution.py:116
  140.2 6.5 %copy.62 = f32[8,1,2,512,128]{4,0,3,2,1:T(8,128)} copy(f32[8,1,2,512,128]{4,3,0,1,2:T(8,128)} %bitcast.209) | data formatting | bytes 8388608 | tf_op jit(solution)/shard_map/transpose | solution.py:38
  146.7 4.6 %copy.59 = bf16[2,8,128,8,128]{4,3,2,1,0:T(8,128)(2,1)} copy(bf16[2,8,128,8,128]{4,3,2,0,1:T(8,128)(2,1)} %bitcast.21) | data formatting | bytes 8388608
  151.3 202.6 %while.35 = (s32[]{:T(128)}, f32[2,4,8,1,128,1]{4,2,1,5,3,0:T(8,128)S(1)}, f32[2,4,8,1,128,128]{5,4,2,1,3,0:T(8,128)}, f32[2,4,8,1,128,1]{4,5,3,2,1,0:T(1,128)S(...) while((s32[]{:T(128)}, ...), condition=%wide.region_13.15_spmd.clone, body=%wide.region_10.14_spmd.clone.sunk | while | flops 4420789760 | bytes 290651552 | solution.py:176
  151.4 3.9 %slice_bitcast_fusion.7 = (bf16[8,128,8,128]{3,2,1,0:T(8,128)(2,1)}, bf16[8,128,8,128]{3,2,1,0:T(8,128)(2,1)S(1)}) fusion(bf16[2,8,128,8,128]{4,3,2,1,0:T(8,128)(2,1)} %get-tuple-element.518), kind=kLoop, calls=%fused_computation.66.clone.1 | loop fusion | bytes 8388608 | tf_op jit(solution)/shard_map/while/body/eval_jaxpr/squeeze | solution.py:150
  155.3 8.9 %gather_fusion = bf16[64,128,8,128]{3,2,1,0:T(8,128)(2,1)} fusion(bf16[8,128,8,128]{3,2,1,0:T(8,128)(2,1)} %get-tuple-element.489, s32[1024]{0:T(1024)S(1)} %pad_clamp_fusion.3), kind=kCustom, calls=%fused_computation.1.clone.clone.1 | custom fusion | bytes 33554688 | tf_op jit(solution)/shard_map/while/body/eval_jaxpr/jit(_take)/gather | solution.py:150
  164.2 7.3 %gather_fusion.1 = bf16[64,128,8,128]{3,2,1,0:T(8,128)(2,1)} fusion(bf16[8,128,8,128]{3,2,1,0:T(8,128)(2,1)S(1)} %get-tuple-element.490, s32[1024]{0:T(1024)S(1)} %pad_clamp_fusion.3), kind=kCustom, calls=%fused_computation.clone.clone.1 | custom fusion | bytes 33554688 | tf_op jit(solution)/shard_map/while/body/eval_jaxpr/jit(_take)/gather | solution.py:147
  171.5 23.2 %broadcast_select_fusion.5 = (bf16[64,128,8,128]{3,2,1,0:T(8,128)(2,1)}, bf16[64,128,8,128]{3,2,1,0:T(8,128)(2,1)}) fusion(bf16[64,128,8,128]{3,2,1,0:T(8,128)(2,1)} %gather_fusion, pred[64]{0:T(512)(128)(4,1)S(1)} %compare_and_fusion.3, bf16[64,128,8,128]{3,2,1,0:T(8,128)(2,1)} %gather_fusion.1), kind=kLoop, calls=%fused_computation.61.clone.1 | loop fusion | flops 16777216 | bytes 67108928 | tf_op jit(solution)/shard_map/while/body/eval_jaxpr/jit(_take)/select_n | solution.py:150
  195.0 19.7 %bitcast_reduce_fusion.2 = (f32[4,8,128]{2,1,0:T(8,128)S(1)}, f32[4,8,2048,128]{3,2,1,0:T(8,128)}) fusion(pred[4,2048]{1,0:T(4,128)(4,1)S(1)} %bitcast.210, bf16[1,4,128,8,1,128]{5,3,2,1,0,4:T(8,128)(2,1)S(1)} %constant_dynamic-slice_fusion.9, bf16[4,2048,8,128]{3,2,1,0:T(8,128)(2,1)} %bitcast.204), kind=kOutput, calls=%fused_computation.47.clone.1 | convolution fusion | flops 2172645376 | bytes 51404800 | tf_op jit(solution)/shard_map/while/body/eval_jaxpr/bqhgd,bkhd->bhgqk/dot_general | solution.py:154
  214.7 15.1 %fusion.72 = f32[4,8,128]{2,1,0:T(8,128)S(1)} fusion(f32[4,8,2048,128]{3,2,1,0:T(8,128)} %get-tuple-element.494, f32[4,8,128]{2,1,0:T(8,128)S(1)} %get-tuple-element.492, pred[4,2048]{1,0:T(4,128)(4,1)S(1)} %bitcast.211), kind=kLoop, calls=%fused_computation.51.clone.1 | loop fusion | flops 41938944 | bytes 33595392 | tf_op jit(solution)/shard_map/while/body/eval_jaxpr/reduce_sum | solution.py:34
  229.8 22.7 %bitcast_dynamic-update-slice_fusion.11 = f32[2,4,8,1,128,128]{5,4,2,1,3,0:T(8,128)} fusion(f32[2,4,8,1,128,128]{5,4,2,1,3,0:T(8,128)} %get-tuple-element.506, s32[]{:T(128)} %get-tuple-element.504, bf16[4,2048,8,128]{3,2,1,0:T(8,128)(2,1)} %bitcast.203, f32[4,8,2048,128]{3,2,1,0:T(8,128)} %get-tuple-element.494, ...), kind=kOutput, calls=%fused_computation.65.clone.1 | convolution fusion | flops 2189426688 | bytes 52462080 | tf_op jit(solution)/shard_map/while/body/eval_jaxpr/bhgqk,bkhd->bhgqd/dot_general | solution.py:163
  252.6 3.9 %slice_bitcast_fusion.7 = (bf16[8,128,8,128]{3,2,1,0:T(8,128)(2,1)}, bf16[8,128,8,128]{3,2,1,0:T(8,128)(2,1)S(1)}) fusion(bf16[2,8,128,8,128]{4,3,2,1,0:T(8,128)(2,1)} %get-tuple-element.518), kind=kLoop, calls=%fused_computation.66.clone.1 | loop fusion | bytes 8388608 | tf_op jit(solution)/shard_map/while/body/eval_jaxpr/squeeze | solution.py:150
  256.5 8.9 %gather_fusion = bf16[64,128,8,128]{3,2,1,0:T(8,128)(2,1)} fusion(bf16[8,128,8,128]{3,2,1,0:T(8,128)(2,1)} %get-tuple-element.489, s32[1024]{0:T(1024)S(1)} %pad_clamp_fusion.3), kind=kCustom, calls=%fused_computation.1.clone.clone.1 | custom fusion | bytes 33554688 | tf_op jit(solution)/shard_map/while/body/eval_jaxpr/jit(_take)/gather | solution.py:150
  265.5 7.4 %gather_fusion.1 = bf16[64,128,8,128]{3,2,1,0:T(8,128)(2,1)} fusion(bf16[8,128,8,128]{3,2,1,0:T(8,128)(2,1)S(1)} %get-tuple-element.490, s32[1024]{0:T(1024)S(1)} %pad_clamp_fusion.3), kind=kCustom, calls=%fused_computation.clone.clone.1 | custom fusion | bytes 33554688 | tf_op jit(solution)/shard_map/while/body/eval_jaxpr/jit(_take)/gather | solution.py:147
  272.9 23.2 %broadcast_select_fusion.5 = (bf16[64,128,8,128]{3,2,1,0:T(8,128)(2,1)}, bf16[64,128,8,128]{3,2,1,0:T(8,128)(2,1)}) fusion(bf16[64,128,8,128]{3,2,1,0:T(8,128)(2,1)} %gather_fusion, pred[64]{0:T(512)(128)(4,1)S(1)} %compare_and_fusion.3, bf16[64,128,8,128]{3,2,1,0:T(8,128)(2,1)} %gather_fusion.1), kind=kLoop, calls=%fused_computation.61.clone.1 | loop fusion | flops 16777216 | bytes 67108928 | tf_op jit(solution)/shard_map/while/body/eval_jaxpr/jit(_take)/select_n | solution.py:150
  296.3 19.7 %bitcast_reduce_fusion.2 = (f32[4,8,128]{2,1,0:T(8,128)S(1)}, f32[4,8,2048,128]{3,2,1,0:T(8,128)}) fusion(pred[4,2048]{1,0:T(4,128)(4,1)S(1)} %bitcast.210, bf16[1,4,128,8,1,128]{5,3,2,1,0,4:T(8,128)(2,1)S(1)} %constant_dynamic-slice_fusion.9, bf16[4,2048,8,128]{3,2,1,0:T(8,128)(2,1)} %bitcast.204), kind=kOutput, calls=%fused_computation.47.clone.1 | convolution fusion | flops 2172645376 | bytes 51404800 | tf_op jit(solution)/shard_map/while/body/eval_jaxpr/bqhgd,bkhd->bhgqk/dot_general | solution.py:154
  316.0 15.1 %fusion.72 = f32[4,8,128]{2,1,0:T(8,128)S(1)} fusion(f32[4,8,2048,128]{3,2,1,0:T(8,128)} %get-tuple-element.494, f32[4,8,128]{2,1,0:T(8,128)S(1)} %get-tuple-element.492, pred[4,2048]{1,0:T(4,128)(4,1)S(1)} %bitcast.211), kind=kLoop, calls=%fused_computation.51.clone.1 | loop fusion | flops 41938944 | bytes 33595392 | tf_op jit(solution)/shard_map/while/body/eval_jaxpr/reduce_sum | solution.py:34
  331.2 22.7 %bitcast_dynamic-update-slice_fusion.11 = f32[2,4,8,1,128,128]{5,4,2,1,3,0:T(8,128)} fusion(f32[2,4,8,1,128,128]{5,4,2,1,3,0:T(8,128)} %get-tuple-element.506, s32[]{:T(128)} %get-tuple-element.504, bf16[4,2048,8,128]{3,2,1,0:T(8,128)(2,1)} %bitcast.203, f32[4,8,2048,128]{3,2,1,0:T(8,128)} %get-tuple-element.494, ...), kind=kOutput, calls=%fused_computation.65.clone.1 | convolution fusion | flops 2189426688 | bytes 52462080 | tf_op jit(solution)/shard_map/while/body/eval_jaxpr/bhgqk,bkhd->bhgqd/dot_general | solution.py:163
  354.6 4.7 %copy.64 = f32[8,8,1,128,128]{4,1,3,0,2:T(8,128)S(1)} copy(f32[8,8,1,128,128]{4,3,1,0,2:T(8,128)} %bitcast.30) | data formatting | bytes 8388608 | tf_op jit(solution)/shard_map/reshape | solution.py:178
  359.3 5.8 %fusion.47 = bf16[1024,8,1,128]{3,1,2,0:T(8,128)(2,1)} fusion(f32[8,1024]{0,1:T(8,128)S(1)} %copy.66, f32[8,1,1024,128]{3,0,1,2:T(8,128)S(1)} %bitcast.207, f32[8,1024]{0,1:T(8,128)S(1)} %copy.63, f32[8,1,1024,128]{3,0,1,2:T(8,128)S(1)} %bitcast.206, f32[8,1024]{0,1:T(8,128)S(1)} %copy.61), kind=kLoop, calls=%fused_computation.91 | loop fusion | flops 5242880 | bytes 10584064 | tf_op jit(solution)/shard_map/convert_element_type | solution.py:188
  (117 shorter events, 25.2 us)
Async XLA Ops:
  1.9 6.1 %collective-permute-start = (bf16[1,1024,8,128]{3,1,2,0:T(8,128)(2,1)S(1)}, bf16[1,1024,8,128]{3,1,2,0:T(8,128)(2,1)}, u32[]{:S(2)}, u32[]{:S(2)}) collective-permute-start(bf16[1,1024,8,128]{3,1,2,0:T(8,128)(2,1)S(1)} %copy.49), channel_id=1, source_target_pairs={{0,1},{1,0},{2,3},{3,2},{4,5},{5,4},{6,7},{7,6},{8,9},{9,8},{10,11... | collective-permute-start | bytes 6291464 | tf_op jit(solution)/shard_map/ppermute | solution.py:21
  7.3 0.6 copy-start.3
  10.8 3.1 copy-start.1
  12.2 39.5 %collective-permute-start.1 = (bf16[2,384,8,128]{3,1,2,0:T(8,128)(2,1)}, bf16[2,384,8,128]{3,1,2,0:T(8,128)(2,1)}, u32[]{:S(2)}, u32[]{:S(2)}) collective-permute-start(bf16[2,384,8,128]{3,1,2,0:T(8,128)(2,1)} %fusion.48), channel_id=1, source_target_pairs={{0,4},{4,8},{8,12},{1,5},{5,9},{9,13},{2,6},{6,10},{10,14},{3,7},{... | collective-permute-start | bytes 4718600 | tf_op jit(solution)/shard_map/ppermute | solution.py:27
  29.1 117.6 %all-to-all-start = ((bf16[4,2,2,128,8,128]{5,4,3,1,2,0:T(8,128)(2,1)}), bf16[4,2,2,128,8,128]{5,4,3,1,2,0:T(8,128)(2,1)}, u32[]{:S(2)}, u32[]{:S(2)}) async-start(bf16[4,2,2,128,8,128]{5,4,3,1,2,0:T(8,128)(2,1)} %pad_maximum_fusion.1), calls=%async_computation | async-start | bytes 8388608 | tf_op jit(solution)/shard_map/all_to_all | solution.py:81
  139.5 11.8 %copy-start.6 = (f32[2,8,1,512,1]{3,1,4,2,0:T(8,128)}, f32[2,8,1,512,1]{3,1,4,2,0:T(8,128)S(1)}, u32[]{:S(2)}) copy-start(f32[2,8,1,512,1]{3,1,4,2,0:T(8,128)S(1)} %get-tuple-element.248) | copy-start | bytes 98308
  146.7 4.6 %copy-start.4 = (f32[2,4,8,1,128,1]{4,2,1,5,3,0:T(8,128)S(1)}, f32[2,4,8,1,128,1]{4,2,1,5,3,0:T(8,128)}, u32[]{:S(2)}) copy-start(f32[2,4,8,1,128,1]{4,2,1,5,3,0:T(8,128)} %copy-done.3) | copy-start | bytes 98308
  151.3 202.6 %copy-start.5 = (f32[1,8,2,512]{3,1,2,0:T(8,128)S(1)}, f32[1,8,2,512]{3,1,2,0:T(8,128)}, u32[]{:S(2)}) copy-start(f32[1,8,2,512]{3,1,2,0:T(8,128)} %copy.72) | copy-start | bytes 98308
  151.3 202.6 %copy-start.7 = (f32[2,8,1,512,1]{3,1,4,2,0:T(8,128)S(1)}, f32[2,8,1,512,1]{3,1,4,2,0:T(8,128)}, u32[]{:S(2)}) copy-start(f32[2,8,1,512,1]{3,1,4,2,0:T(8,128)} %copy-done.6) | copy-start | bytes 98308
  171.5 23.4 %copy-start = (bf16[2,4,128,8,1,128]{5,3,2,1,0,4:T(8,128)(2,1)S(1)}, bf16[2,4,128,8,1,128]{5,3,2,1,0,4:T(8,128)(2,1)}, u32[]{:S(2)}) copy-start(bf16[2,4,128,8,1,128]{5,3,2,1,0,4:T(8,128)(2,1)} %get-tuple-element.520) | copy-start | bytes 6291460 | tf_op jit(solution)/shard_map/while
  272.9 23.4 %copy-start = (bf16[2,4,128,8,1,128]{5,3,2,1,0,4:T(8,128)(2,1)S(1)}, bf16[2,4,128,8,1,128]{5,3,2,1,0,4:T(8,128)(2,1)}, u32[]{:S(2)}) copy-start(bf16[2,4,128,8,1,128]{5,3,2,1,0,4:T(8,128)(2,1)} %get-tuple-element.520) | copy-start | bytes 6291460 | tf_op jit(solution)/shard_map/while
  354.6 4.7 %copy-start.2 = (f32[8,1,2,512,128]{4,0,3,2,1:T(8,128)S(1)}, f32[8,1,2,512,128]{4,0,3,2,1:T(8,128)}, u32[]{:S(2)}) copy-start(f32[8,1,2,512,128]{4,0,3,2,1:T(8,128)} %copy.62) | copy-start | bytes 12582916
